TPU v7x, 32 devices: a whole 2x2x4 slice. The times are simulated.
32 devices in a mesh: fsdp: 16 (over z, y, core), sp: 2 (over x).
Axes of the slice: x: 2, y: 2, z: 4, core: 2. Of those that a mesh axis runs over, the one named last changes fastest.
Arguments:
- latents: bfloat16 [32, 256, 768], P('fsdp', 'sp'), may hold values from -6 to 6
- condition: bfloat16 [32, 768], P('fsdp'), may hold values from -6 to 6
- cotangent: bfloat16 [32, 256, 768], P('fsdp', 'sp'), may hold values from -6 to 6
- w_ada: bfloat16 [768, 4608], P('fsdp'), may hold values from -0.21875 to 0.21875
- b_ada: bfloat16 [4608], P('fsdp'), may hold values from -3 to 3
- w_qkv: bfloat16 [768, 2304], P('fsdp'), may hold values from -0.21875 to 0.21875
- b_query: bfloat16 [768], P('fsdp'), may hold values from -3 to 3
- b_value: bfloat16 [768], P('fsdp'), may hold values from -3 to 3
- w_out: bfloat16 [768, 768], P('fsdp'), may hold values from -0.875 to 0.875
- b_out: bfloat16 [768], P('fsdp'), may hold values from -3 to 3
- w_up: bfloat16 [768, 3072], P('fsdp'), may hold values from -0.21875 to 0.21875
- b_up: bfloat16 [3072], P('fsdp'), may hold values from -3 to 3
- w_down: bfloat16 [3072, 768], P('fsdp'), may hold values from -0.109375 to 0.109375
- b_down: bfloat16 [768], P('fsdp'), may hold values from -3 to 3
Outputs:
- output: bfloat16 [32, 256, 768], P('fsdp', 'sp')
- grad_latents: float32 [32, 256, 768], P('fsdp', 'sp')
- grad_condition: float32 [32, 768], P('fsdp')
- grad_w_ada: float32 [768, 4608], P(('fsdp', 'sp'))
- grad_b_ada: float32 [4608], P(('fsdp', 'sp'))
- grad_w_qkv: float32 [768, 2304], P(('fsdp', 'sp'))
- grad_b_query: float32 [768], P(('fsdp', 'sp'))
- grad_b_value: float32 [768], P(('fsdp', 'sp'))
- grad_w_out: float32 [768, 768], P(('fsdp', 'sp'))
- grad_b_out: float32 [768], P(('fsdp', 'sp'))
- grad_w_up: float32 [768, 3072], P(('fsdp', 'sp'))
- grad_b_up: float32 [3072], P(('fsdp', 'sp'))
- grad_w_down: float32 [3072, 768], P(('fsdp', 'sp'))
- grad_b_down: float32 [768], P(('fsdp', 'sp'))
All inputs are finite; a program needn't handle non-finite values.
Results may differ from a plain program's by a relative error of at most 0.015.
The roundings to bfloat16 on the way count: a program that leaves them out, or rounds other values in their place, can miss the bound.
Values may be sent and summed in bfloat16 or wider, within the bound.
A program may use at most 256 MiB of HBM per device.

v0:
```python
import jax
import jax.numpy as jnp
from jax import lax
from jax.sharding import PartitionSpec as P

D = 768
H = 12
HD = 64
eps = 1e-06


def normalize(values):
    centered = values - jnp.mean(values, axis=-1, keepdims=True)
    inverse = lax.rsqrt(jnp.mean(centered * centered, axis=-1, keepdims=True) + eps)
    return (centered * inverse, inverse)


def norm_back(grad_in, normed, inverse):
    return inverse * (
        grad_in
        - jnp.mean(grad_in, axis=-1, keepdims=True)
        - normed * jnp.mean(grad_in * normed, axis=-1, keepdims=True)
    )


def gelu_tanh(values):
    return jax.nn.gelu(values, approximate=True)


def silu_back(values, grad_out):
    return jax.vjp(jax.nn.silu, values)[1](grad_out)[0]


def gelu_back(values, grad_out):
    return jax.vjp(gelu_tanh, values)[1](grad_out)[0]


LANES = 2048


def body(
    latents,
    condition,
    cotangent,
    w_ada,
    b_ada,
    w_qkv,
    b_query,
    b_value,
    w_out,
    b_out,
    w_up,
    b_up,
    w_down,
    b_down,
):
    f32 = jnp.float32
    bf16 = jnp.bfloat16
    fsdp_count = lax.axis_size("fsdp")
    sp_count = lax.axis_size("sp")
    owners = fsdp_count * sp_count
    fsdp_index = lax.axis_index("fsdp")
    sp_index = lax.axis_index("sp")
    owner_index = fsdp_index * sp_count + sp_index
    pair_latents = latents.shape[0]
    own_latents = pair_latents // sp_count
    latent_total = pair_latents * fsdp_count
    tokens_all = latents.shape[1] * sp_count
    scale_factor = HD ** (-0.5)
    small = [condition.reshape(-1), b_ada, b_query, b_value, b_out, b_up, b_down]
    width = sum((part.size for part in small))
    padded = -(-width // LANES) * LANES
    small.append(jnp.zeros((padded - width,), bf16))
    small_all = lax.all_gather(
        jnp.concatenate(small).reshape(1, padded // 128, 128), "fsdp", axis=0, tiled=True
    ).reshape(fsdp_count, padded)
    pieces = []
    start = 0
    for part in small[:-1]:
        pieces.append(small_all[:, start : start + part.size].reshape(-1))
        start = start + part.size
    cond_all, ada_bias, query_bias, value_bias, out_bias, up_bias, down_bias = pieces
    cond_all = cond_all.reshape(latent_total, D).astype(f32)
    silu_all = jax.nn.silu(cond_all)
    inputs = lax.all_to_all(latents, "sp", split_axis=0, concat_axis=1, tiled=True).astype(f32)
    grad_out = lax.all_to_all(cotangent, "sp", split_axis=0, concat_axis=1, tiled=True).astype(f32)
    ada_rows = w_ada.shape[0]
    silu_mine = lax.dynamic_index_in_dim(
        silu_all.astype(bf16).reshape(fsdp_count, sp_count, own_latents, D), sp_index, 1, False
    )
    silu_mine = lax.dynamic_index_in_dim(
        silu_mine.reshape(fsdp_count * own_latents, fsdp_count, ada_rows), fsdp_index, 1, False
    )
    mod_part = jnp.dot(silu_mine, w_ada, preferred_element_type=f32)
    mod_part = lax.all_to_all(
        mod_part.reshape(fsdp_count, own_latents * 6 * D),
        "fsdp",
        split_axis=0,
        concat_axis=0,
        tiled=True,
    )
    modulate = jnp.sum(mod_part, axis=0).reshape(own_latents, 6 * D) + ada_bias.astype(f32)
    mod_parts = modulate.reshape(own_latents, 6, 1, D)
    shift_one, scale_one, gate_one = (mod_parts[:, 0], mod_parts[:, 1], mod_parts[:, 2])
    shift_two, scale_two, gate_two = (mod_parts[:, 3], mod_parts[:, 4], mod_parts[:, 5])
    qkv_full = lax.all_gather(w_qkv, "fsdp", axis=0, tiled=True)
    out_full = lax.all_gather(w_out, "fsdp", axis=0, tiled=True)
    up_full = lax.all_gather(w_up, "fsdp", axis=0, tiled=True)
    down_full = lax.all_gather(w_down, "fsdp", axis=0, tiled=True)
    normed_one, inverse_one = normalize(inputs)
    attn_in = (normed_one * (1.0 + scale_one) + shift_one).astype(bf16)
    qkv_bias = jnp.concatenate([query_bias, jnp.zeros_like(query_bias), value_bias]).astype(f32)
    projected = (
        jnp.einsum("btd,de->bte", attn_in, qkv_full, preferred_element_type=f32) + qkv_bias
    ).astype(bf16)
    heads = projected.reshape(own_latents, tokens_all, 3, H, HD).transpose(2, 0, 3, 1, 4)
    queries, key_heads, value_heads = (heads[0], heads[1], heads[2])
    scores = (
        jnp.einsum("bhqd,bhkd->bhqk", queries, key_heads, preferred_element_type=f32) * scale_factor
    )
    log_total = jnp.log(jnp.sum(jnp.exp(scores), axis=-1, keepdims=True))
    soft_float = jnp.exp(scores - log_total)
    soft_half = soft_float.astype(bf16)
    mixed = jnp.einsum(
        "bhqk,bhkd->bhqd", soft_half, value_heads, preferred_element_type=f32
    ).astype(bf16)
    mixed_tokens = mixed.transpose(0, 2, 1, 3).reshape(own_latents, tokens_all, D)
    attn_proj = jnp.einsum(
        "btd,de->bte", mixed_tokens, out_full, preferred_element_type=f32
    ) + out_bias.astype(f32)
    residual = inputs + gate_one * attn_proj
    normed_two, inverse_two = normalize(residual)
    mlp_in = (normed_two * (1.0 + scale_two) + shift_two).astype(bf16)
    up_value = jnp.einsum(
        "btd,df->btf", mlp_in, up_full, preferred_element_type=f32
    ) + up_bias.astype(f32)
    activated = gelu_tanh(up_value).astype(bf16)
    down_value = jnp.einsum(
        "btf,fd->btd", activated, down_full, preferred_element_type=f32
    ) + down_bias.astype(f32)
    output = (residual + gate_two * down_value).astype(bf16)
    output = lax.all_to_all(output, "sp", split_axis=1, concat_axis=0, tiled=True)
    grad_gate_two = jnp.sum(grad_out * down_value, axis=1)
    grad_down = (grad_out * gate_two).astype(bf16)
    gw_down = jnp.einsum("btf,btd->fd", activated, grad_down, preferred_element_type=f32)
    gb_down = jnp.sum(grad_down.astype(f32), axis=(0, 1))
    grad_act = jnp.einsum("btd,fd->btf", grad_down, down_full, preferred_element_type=f32)
    grad_up = gelu_back(up_value, grad_act).astype(bf16)
    gw_up = jnp.einsum("btd,btf->df", mlp_in, grad_up, preferred_element_type=f32)
    gb_up = jnp.sum(grad_up.astype(f32), axis=(0, 1))
    grad_mlp = jnp.einsum("btf,df->btd", grad_up, up_full, preferred_element_type=f32)
    grad_scale_two = jnp.sum(grad_mlp * normed_two, axis=1)
    grad_shift_two = jnp.sum(grad_mlp, axis=1)
    grad_resid = grad_out + norm_back(grad_mlp * (1.0 + scale_two), normed_two, inverse_two)
    grad_gate_one = jnp.sum(grad_resid * attn_proj, axis=1)
    grad_proj = (grad_resid * gate_one).astype(bf16)
    gw_out = jnp.einsum("btd,bte->de", mixed_tokens, grad_proj, preferred_element_type=f32)
    gb_out = jnp.sum(grad_proj.astype(f32), axis=(0, 1))
    grad_mixed = jnp.einsum("bte,de->btd", grad_proj, out_full, preferred_element_type=f32).astype(
        bf16
    )
    grad_heads = grad_mixed.reshape(own_latents, tokens_all, H, HD).transpose(0, 2, 1, 3)
    grad_soft = jnp.einsum("bhqd,bhkd->bhqk", grad_heads, value_heads, preferred_element_type=f32)
    delta_sum = jnp.sum(soft_float * grad_soft, axis=-1, keepdims=True)
    grad_scores = (soft_float * (grad_soft - delta_sum)).astype(bf16)
    grad_queries = (
        jnp.einsum("bhqk,bhkd->bhqd", grad_scores, key_heads, preferred_element_type=f32)
        * scale_factor
    ).astype(bf16)
    grad_keys = (
        jnp.einsum("bhqk,bhqd->bhkd", grad_scores, queries, preferred_element_type=f32)
        * scale_factor
    ).astype(bf16)
    grad_values = jnp.einsum(
        "bhqk,bhqd->bhkd", soft_half, grad_heads, preferred_element_type=f32
    ).astype(bf16)
    grad_tokens = (
        jnp.stack([grad_queries, grad_keys, grad_values], axis=0)
        .transpose(1, 3, 0, 2, 4)
        .reshape(own_latents, tokens_all, 3 * D)
    )
    gw_qkv = jnp.einsum("btd,bte->de", attn_in, grad_tokens, preferred_element_type=f32)
    grad_tok_float = grad_tokens.astype(f32)
    gb_query = jnp.sum(grad_tok_float[:, :, :D], axis=(0, 1))
    gb_value = jnp.sum(grad_tok_float[:, :, 2 * D :], axis=(0, 1))
    grad_attn_in = jnp.einsum("bte,de->btd", grad_tokens, qkv_full, preferred_element_type=f32)
    grad_scale_one = jnp.sum(grad_attn_in * normed_one, axis=1)
    grad_shift_one = jnp.sum(grad_attn_in, axis=1)
    grad_latents = grad_resid + norm_back(grad_attn_in * (1.0 + scale_one), normed_one, inverse_one)
    grad_latents = lax.all_to_all(grad_latents, "sp", split_axis=1, concat_axis=0, tiled=True)
    grad_mod = jnp.concatenate(
        [
            grad_shift_one,
            grad_scale_one,
            grad_gate_one,
            grad_shift_two,
            grad_scale_two,
            grad_gate_two,
        ],
        axis=1,
    )
    grad_mod = lax.all_to_all(
        jnp.broadcast_to(grad_mod[None], (owners, own_latents, 6 * D)),
        ("fsdp", "sp"),
        split_axis=0,
        concat_axis=0,
        tiled=True,
    ).reshape(latent_total, 6 * D)
    rows = D // owners
    biases = (gb_query, gb_value, gb_out, gb_up, gb_down)
    bias_rows = jnp.concatenate([part.reshape(owners, -1) for part in biases], axis=1)
    bias_width = bias_rows.shape[1]
    bias_lanes = -(-bias_width // (rows * 128)) * 128
    bias_rows = jnp.pad(bias_rows, ((0, 0), (0, rows * bias_lanes - bias_width)))
    stack = down_full.shape[0] // D
    gw_down = (
        gw_down.astype(bf16)
        .reshape(owners, stack, rows, D)
        .transpose(0, 2, 1, 3)
        .reshape(D, stack * D)
    )
    packed = jnp.concatenate(
        [
            gw_down,
            gw_up.astype(bf16),
            gw_qkv.astype(bf16),
            gw_out.astype(bf16),
            bias_rows.astype(bf16).reshape(D, bias_lanes),
        ],
        axis=1,
    )
    owned = lax.psum_scatter(packed, ("fsdp", "sp"), scatter_dimension=0, tiled=True).astype(f32)
    own_weights = []
    start = 0
    for width in (stack * D, up_full.shape[1], 3 * D, D, bias_lanes):
        own_weights.append(owned[:, start : start + width])
        start = start + width
    own_down, own_up, own_qkv, own_out, bias_sums = own_weights
    own_down = own_down.reshape(rows, stack, D).transpose(1, 0, 2).reshape(stack * rows, D)
    bias_sums = bias_sums.reshape(-1)
    own_bias = []
    start = 0
    for part in biases:
        width = part.size // owners
        own_bias.append(bias_sums[start : start + width])
        start = start + width
    own_gb_query, own_gb_value, own_gb_out, own_gb_up, own_gb_down = own_bias
    silu_rows = lax.dynamic_index_in_dim(
        silu_all.reshape(latent_total, owners, D // owners), owner_index, 1, False
    )
    own_ada = jnp.dot(silu_rows.T, grad_mod, precision=lax.Precision.HIGHEST)
    own_gb_ada = lax.dynamic_index_in_dim(
        jnp.sum(grad_mod, axis=0).reshape(owners, -1), owner_index, 0, False
    )
    grad_silu = jnp.dot(grad_mod.astype(bf16), w_ada.T, preferred_element_type=f32)
    grad_silu = lax.all_to_all(
        grad_silu.reshape(fsdp_count, pair_latents * ada_rows),
        "fsdp",
        split_axis=0,
        concat_axis=0,
        tiled=True,
    )
    grad_silu = (
        grad_silu.reshape(fsdp_count, pair_latents, ada_rows)
        .transpose(1, 0, 2)
        .reshape(pair_latents, D)
    )
    grad_condition = silu_back(condition.astype(f32), grad_silu)
    return (
        output,
        grad_latents,
        grad_condition,
        own_ada,
        own_gb_ada,
        own_qkv,
        own_gb_query,
        own_gb_value,
        own_out,
        own_gb_out,
        own_up,
        own_gb_up,
        own_down,
        own_gb_down,
    )


def solution(mesh):
    in_specs = (
        P("fsdp", "sp", None),
        P("fsdp", None),
        P("fsdp", "sp", None),
        P("fsdp", None),
        P("fsdp"),
        P("fsdp", None),
        P("fsdp"),
        P("fsdp"),
        P("fsdp", None),
        P("fsdp"),
        P("fsdp", None),
        P("fsdp"),
        P("fsdp", None),
        P("fsdp"),
    )
    out_specs = (
        P("fsdp", "sp", None),
        P("fsdp", "sp", None),
        P("fsdp", None),
        P(("fsdp", "sp"), None),
        P(("fsdp", "sp")),
        P(("fsdp", "sp"), None),
        P(("fsdp", "sp")),
        P(("fsdp", "sp")),
        P(("fsdp", "sp"), None),
        P(("fsdp", "sp")),
        P(("fsdp", "sp"), None),
        P(("fsdp", "sp")),
        P(("fsdp", "sp"), None),
        P(("fsdp", "sp")),
    )
    return jax.shard_map(body, mesh=mesh, in_specs=in_specs, out_specs=out_specs, check_vma=False)
```

profile of v0, /device:TPU:0, one launch (start us, length us, event | category | flops | bytes accessed | tf_op | source)
XLA Modules:
  0.0 443.4 jit_solution(5523221434767197551)
XLA Ops:
  8.0 0.7 all-gather.7.cloned.1.call-update
  10.0 4.2 all-to-all-start
  14.2 0.7 reshape.728
  14.9 4.1 concatenate.24
  19.1 22.7 %all_gather.15 = bf16[16,32,128]{2,1,0:T(8,128)(2,1)S(1)} all-gather(bf16[1,32,128]{2,1,0:T(8,128)(2,1)S(1)} %bitcast.188), channel_id=1, replica_groups=mesh['fsdp'=16,'sp'=2] {'fsdp'}, dimensions={0}, use_global_device_ids=true | all-gather | bytes 139264 | tf_op jit(solution)/shard_map/all_gather | solution.py:74
  42.6 1.0 copy.104
  43.7 3.5 all-to-all-start.1
  48.0 13.7 %all-to-all-done.1 = f32[16,1,4608]{2,1,0:T(1,128)S(1)} async-done(((f32[16,1,4608]{2,1,0:T(1,128)}), f32[16,1,4608]{2,1,0:T(1,128)S(1)}, u32[]{:S(2)}, u32[]{:S(2)}) %all-to-all-start.1) | async-done | bytes 294944 | tf_op jit(solution)/shard_map/all_to_all | solution.py:95
  61.7 3.8 all-to-all-start.3
  65.8 6.4 %all-to-all-done.3 = bf16[2,128,768]{2,1,0:T(8,128)(2,1)S(1)} async-done(((bf16[2,128,768]{2,1,0:T(8,128)(2,1)}), bf16[2,128,768]{2,1,0:T(8,128)(2,1)S(1)}, u32[]{:S(2)}, u32[]{:S(2)}) %all-to-all-start.3) | async-done | bytes 393248 | tf_op jit(solution)/shard_map/all_to_all | solution.py:86
  72.4 0.8 fusion.24
  73.5 1.0 fusion.43
  74.5 4.1 fusion.3
  78.6 1.6 copy.105
  80.2 2.4 fusion.60
  82.6 4.9 %convolution_convert_fusion.4 = bf16[12,256,64]{1,2,0:T(8,128)(2,1)} fusion(f32[12,256,256]{1,2,0:T(8,128)} %fusion.60, bf16[3,1,12,256,64]{3,4,2,1,0:T(8,128)(2,1)S(1)} %bitcast.160), kind=kOutput, calls=%fused_computation.34 | convolution fusion | flops 104008960 | bytes 7077888 | tf_op jit(solution)/shard_map/bhqk,bhkd->bhqd/dot_general | solution.py:124
  87.4 17.1 %all-gather.7.cloned.1.call-done = bf16[768,768]{1,0:T(8,128)(2,1)} async-done(((bf16[48,768]{1,0:T(8,128)(2,1)}), bf16[768,768]{1,0:T(8,128)(2,1)}) %all-gather.7.cloned.1.call-update) | async-done | bytes 1179664 | tf_op jit(solution)/shard_map/all_gather | solution.py:107
  104.6 2.8 fusion.83
  107.6 51.3 %all-gather.11.cloned.1.call-done = bf16[3072,768]{1,0:T(8,128)(2,1)} async-done(((bf16[192,768]{1,0:T(8,128)(2,1)}), bf16[3072,768]{1,0:T(8,128)(2,1)}) %all-gather.11.cloned.1.call-update) | async-done | bytes 4718608 | tf_op jit(solution)/shard_map/all_gather | solution.py:109
  158.9 5.6 %fusion.86 = f32[256,3072]{1,0:T(8,128)} fusion(bf16[256,768]{1,0:T(8,128)(2,1)} %fusion.24, bf16[3072,768]{1,0:T(8,128)(2,1)} %all-gather.11.cloned.1.call-done), kind=kOutput, calls=%fused_computation.159 | convolution fusion | flops 1207959552 | bytes 8257536 | tf_op jit(solution)/shard_map/btd,fd->btf/dot_general | solution.py:147
  164.5 48.2 %all-gather.9.cloned.1.call-done = bf16[768,3072]{1,0:T(8,128)(2,1)} async-done(((bf16[48,3072]{1,0:T(8,128)(2,1)}), bf16[768,3072]{1,0:T(8,128)(2,1)}) %all-gather.9.cloned.1.call-update) | async-done | bytes 4718608 | tf_op jit(solution)/shard_map/all_gather | solution.py:108
  212.7 7.0 %fusion.80 = (bf16[3072]{0:T(1024)(128)(2,1)S(1)}, bf16[256,3072]{1,0:T(8,128)(2,1)S(1)}, f32[256,3072]{1,0:T(8,128)S(1)}) fusion(f32[256,3072]{1,0:T(8,128)} %fusion.86, f32[3072]{0:T(1024)S(1)} %reshape.760, bf16[768,3072]{1,0:T(8,128)(2,1)} %all-gather.9.cloned.1.call-done, f32[256,768]{1,0:T(8,128)S(1)} %get-tuple-element.36, ...), kind=kOutput, calls=%fused_computation.153 | convolution fusion | flops 1226241024 | bytes 13395968 | tf_op jit(solution)/shard_map/btd,df->btf/dot_general | solution.py:134
  219.8 1.4 fusion.87
  221.2 0.9 copy-done.19
  222.1 1.7 copy-done.2
  223.8 2.9 fusion.25
  226.7 1.3 fusion.82
  228.0 0.8 copy-done.5
  229.3 0.9 copy.109
  230.2 5.0 %fusion.20 = bf16[1,1,12,256,64]{3,4,2,1,0:T(8,128)(2,1)} fusion(bf16[12,256,64]{1,2,0:T(8,128)(2,1)} %bitcast.174, f32[12,256,256]{1,2,0:T(8,128)} %fusion.60), kind=kOutput, calls=%fused_computation.39 | convolution fusion | flops 104008960 | bytes 3932160 | tf_op jit(solution)/shard_map/bhqk,bhqd->bhkd/dot_general | solution.py:174
  235.8 1.3 copy-done.1
  237.1 2.9 multiply_reduce_fusion
  240.6 1.4 fusion.22
  241.9 1.1 fusion.21
  243.1 4.4 convolution_convert_fusion.2
  247.7 1.2 pad_maximum_fusion
  249.8 4.7 %copy.117 = bf16[32,24,4,768]{3,2,1,0:T(4,128)(2,1)S(1)} copy(bf16[32,24,4,768]{3,1,2,0:T(8,128)(2,1)} %bitcast.167) | data formatting | bytes 9437184 | tf_op jit(solution)/shard_map/transpose | solution.py:219
  254.5 1.0 copy.132
  255.6 2.5 constant_dynamic-update-slice_fusion.7
  258.0 3.7 fusion.2
  261.8 2.9 fusion.1
  264.7 1.6 fusion.17
  267.0 1.0 copy-done.14
  269.1 3.3 reduce.65
  272.3 0.8 reshape.781
  273.2 3.6 all-to-all-start.2
  276.8 3.9 fusion.39
  281.1 1.7 copy.113
  282.8 1.2 all-to-all-done.2
  284.0 3.6 all-to-all-start.4
  287.7 10.6 %all-to-all-done.4 = f32[1,256,768]{2,0,1:T(1,128)S(1)} async-done(((f32[1,256,768]{2,0,1:T(1,128)}), f32[1,256,768]{2,0,1:T(1,128)S(1)}, u32[]{:S(2)}, u32[]{:S(2)}) %all-to-all-start.4) | async-done | bytes 786464 | tf_op jit(solution)/shard_map/all_to_all | solution.py:190
  298.2 1.1 broadcast_in_dim.11
  299.4 2.6 all-to-all-start.5
  302.8 0.8 copy.126
  303.6 0.9 copy.127
  304.5 18.4 %all-to-all-done.5 = f32[32,1,4608]{2,1,0:T(1,128)S(1)} async-done(((f32[32,1,4608]{2,1,0:T(1,128)}), f32[32,1,4608]{2,1,0:T(1,128)S(1)}, u32[]{:S(2)}, u32[]{:S(2)}) %all-to-all-start.5) | async-done | bytes 589856 | tf_op jit(solution)/shard_map/all_to_all | solution.py:202
  323.9 3.5 all-to-all-start.6
  327.8 1.3 fusion.46
  329.7 6.0 %all-to-all-done.6 = f32[16,1,96]{2,1,0:T(1,128)S(1)} async-done(((f32[16,1,96]{2,1,0:T(1,128)}), f32[16,1,96]{2,1,0:T(1,128)S(1)}, u32[]{:S(2)}, u32[]{:S(2)}) %all-to-all-start.6) | async-done | bytes 6176 | tf_op jit(solution)/shard_map/all_to_all | solution.py:256
  337.6 92.9 %reduce-scatter.4.cloned.1.call-done = bf16[24,9344]{1,0:T(8,128)(2,1)} async-done(((bf16[768,9344]{1,0:T(8,128)(2,1)}), bf16[24,9344]{1,0:T(8,128)(2,1)}) %reduce-scatter.4.cloned.1.call-update) | async-done | bytes 448528
  430.5 1.1 convert_element_type.313
  432.8 1.7 fusion.84
  434.7 0.8 copy.119
  436.1 0.7 slice.130
  (128 shorter events, 16.4 us)
Async XLA Ops:
  7.2 35.3 %copy-start = (bf16[48,4608]{1,0:T(8,128)(2,1)S(1)}, bf16[48,4608]{1,0:T(8,128)(2,1)}, u32[]{:S(2)}) copy-start(bf16[48,4608]{1,0:T(8,128)(2,1)} %param.17) | copy-start | bytes 1327108
  7.2 67.3 %all-gather.5.cloned.1.call-start = ((), (), s32[]{:S(2)}) async-start(), calls=%async_computation.8 | async-start | bytes 3760128 | tf_op jit(solution)/shard_map/all_gather | solution.py:106
  7.9 96.6 %all-gather.7.cloned.1.call-start = ((), (), s32[]{:S(2)}) async-start(), calls=%async_computation.9 | async-start | bytes 1253376 | tf_op jit(solution)/shard_map/all_gather | solution.py:107
  8.7 150.2 %all-gather.11.cloned.1.call-start = ((), (), s32[]{:S(2)}) async-start(), calls=%async_computation.11 | async-start | bytes 5013504 | tf_op jit(solution)/shard_map/all_gather | solution.py:109
  9.4 203.3 %all-gather.9.cloned.1.call-start = ((), (), s32[]{:S(2)}) async-start(), calls=%async_computation.10 | async-start | bytes 5013504 | tf_op jit(solution)/shard_map/all_gather | solution.py:108
  10.0 33.7 %all-to-all-start = ((bf16[2,128,768]{2,1,0:T(8,128)(2,1)}), bf16[2,128,768]{2,1,0:T(8,128)(2,1)S(1)}, u32[]{:S(2)}, u32[]{:S(2)}) async-start(bf16[2,128,768]{2,1,0:T(8,128)(2,1)} %param.14), calls=%async_computation | async-start | bytes 786432 | tf_op jit(solution)/shard_map/all_to_all | solution.py:85
  43.7 18.0 %all-to-all-start.1 = ((f32[16,1,4608]{2,1,0:T(1,128)}), f32[16,1,4608]{2,1,0:T(1,128)S(1)}, u32[]{:S(2)}, u32[]{:S(2)}) async-start(f32[16,1,4608]{2,1,0:T(1,128)} %copy.104), calls=%async_computation.1 | async-start | bytes 589824 | tf_op jit(solution)/shard_map/all_to_all | solution.py:95
  61.7 10.5 %all-to-all-start.3 = ((bf16[2,128,768]{2,1,0:T(8,128)(2,1)}), bf16[2,128,768]{2,1,0:T(8,128)(2,1)S(1)}, u32[]{:S(2)}, u32[]{:S(2)}) async-start(bf16[2,128,768]{2,1,0:T(8,128)(2,1)} %param.16), calls=%async_computation.3 | async-start | bytes 786432 | tf_op jit(solution)/shard_map/all_to_all | solution.py:86
  65.5 365.0 %reduce-scatter.4.cloned.1.call-start = ((), (), s32[]{:S(2)}) async-start(), calls=%async_computation.12 | async-start | bytes 14800896
  212.7 7.0 %copy-start.16 = (bf16[768,3072]{1,0:T(8,128)(2,1)S(1)}, bf16[768,3072]{1,0:T(8,128)(2,1)}, u32[]{:S(2)}) copy-start(bf16[768,3072]{1,0:T(8,128)(2,1)} %all-gather.9.cloned.1.call-done) | copy-start | bytes 14155780
  219.7 1.5 copy-start.17
  219.8 2.4 copy-start.19
  219.8 4.0 copy-start.2
  226.7 2.0 copy-start.3
  228.0 0.8 copy-start.5
  230.2 5.0 %copy-start.12 = (bf16[256,768]{0,1:T(8,128)(2,1)S(1)}, bf16[256,768]{0,1:T(8,128)(2,1)}, u32[]{:S(2)}) copy-start(bf16[256,768]{0,1:T(8,128)(2,1)} %copy.109) | copy-start | bytes 1179652
  235.2 1.9 copy-start.1
  240.5 2.5 copy-start.9
  240.6 2.5 copy-start.20
  243.1 4.6 %copy-start.10 = (bf16[1,1,12,256,64]{3,4,2,1,0:T(8,128)(2,1)S(1)}, bf16[1,1,12,256,64]{3,4,2,1,0:T(8,128)(2,1)}, u32[]{:S(2)}) copy-start(bf16[1,1,12,256,64]{3,4,2,1,0:T(8,128)(2,1)} %fusion.22) | copy-start | bytes 1179652
  255.6 2.5 copy-start.18
  258.0 3.7 copy-start.13
  261.8 2.9 copy-start.6
  261.8 2.9 copy-start.11
  267.0 1.0 copy-start.14
  273.2 10.8 %all-to-all-start.2 = ((bf16[2,2,49152]{2,1,0:T(2,128)(2,1)}), bf16[2,2,49152]{2,1,0:T(2,128)(2,1)S(1)}, u32[]{:S(2)}, u32[]{:S(2)}) async-start(bf16[2,2,49152]{2,1,0:T(2,128)(2,1)} %reshape.781), calls=%async_computation.2 | async-start | bytes 786432 | tf_op jit(solution)/shard_map/all_to_all | solution.py:142
  276.8 4.0 copy-start.7
  276.8 4.0 copy-start.8
  284.0 14.2 %all-to-all-start.4 = ((f32[1,256,768]{2,0,1:T(1,128)}), f32[1,256,768]{2,0,1:T(1,128)S(1)}, u32[]{:S(2)}, u32[]{:S(2)}) async-start(f32[1,256,768]{2,0,1:T(1,128)} %copy.113), calls=%async_computation.4 | async-start | bytes 1572864 | tf_op jit(solution)/shard_map/all_to_all | solution.py:190
  299.4 23.6 %all-to-all-start.5 = ((f32[32,1,4608]{2,1,0:T(1,128)}), f32[32,1,4608]{2,1,0:T(1,128)S(1)}, u32[]{:S(2)}, u32[]{:S(2)}) async-start(f32[32,1,4608]{2,1,0:T(1,128)} %broadcast_in_dim.11), calls=%async_computation.5 | async-start | bytes 1179648 | tf_op jit(solution)/shard_map/all_to_all | solution.py:202
  302.4 34.6 %copy-start.15 = (bf16[2,768]{1,0:T(2,128)(2,1)S(1)}, bf16[2,768]{1,0:T(2,128)(2,1)}, u32[]{:S(2)}) copy-start(bf16[2,768]{1,0:T(2,128)(2,1)} %param.15) | copy-start | bytes 9220
  323.9 11.8 %all-to-all-start.6 = ((f32[16,1,96]{2,1,0:T(1,128)}), f32[16,1,96]{2,1,0:T(1,128)S(1)}, u32[]{:S(2)}, u32[]{:S(2)}) async-start(f32[16,1,96]{2,1,0:T(1,128)} %bitcast.29), calls=%async_computation.6 | async-start | bytes 16384 | tf_op jit(solution)/shard_map/all_to_all | solution.py:256
  430.5 5.0 %copy-start.4 = (bf16[24,9344]{1,0:T(8,128)(2,1)S(1)}, bf16[24,9344]{1,0:T(8,128)(2,1)}, u32[]{:S(2)}) copy-start(bf16[24,9344]{1,0:T(8,128)(2,1)} %reduce-scatter.4.cloned.1.call-done) | copy-start | bytes 1345540
Sparse Core Ops, SparseCore 0:
  10.3 55.0 all-gather.4
  67.7 36.8 all-gather.6
  106.9 51.9 all-gather.10
  161.0 51.6 all-gather.8
  267.1 163.3 reduce-scatter.3
where the time goes:
time: 444 us; the launch traced here: 443 us
  waiting for transfers between devices  268 us (60%)
  matrix products  58 us (13%)
  local copies, waits for them, and re-layouts  38.8 us (9%)
  starting transfers between devices  24.9 us (6%)
  blocking collectives  22.7 us (5%)
  other arithmetic  16.2 us (4%)
  between operations  14.4 us (3%)
    unnamed x6, waiting for transfers between devices  95.5 us
    all_gather x1, waiting for transfers between devices, body(): down_full = lax.all_gather(w_down, 'fsdp', axis=0, tiled=True)  51.3 us
    all_gather x1, waiting for transfers between devices, body(): up_full = lax.all_gather(w_up, 'fsdp', axis=0, tiled=True)  48.2 us
    all_gather x1, blocking collectives, body(): lax.all_gather(jnp.concatenate(small).reshape(1, padded // 128, 128), 'fs...  22.7 us
    all_to_all x1, waiting for transfers between devices, body(): lax.all_to_all(jnp.broadcast_to(grad_mod[None], (owners, own_latents, 6 *...  18.4 us
    all_gather x1, waiting for transfers between devices, body(): out_full = lax.all_gather(w_out, 'fsdp', axis=0, tiled=True)  17.1 us
    all_to_all x1, waiting for transfers between devices, body(): lax.all_to_all(mod_part.reshape(fsdp_count, own_latents * 6 * D), 'fsdp',...  13.7 us
    unnamed x55, local copies, waits for them, and re-layouts  12.7 us
  transfers between devices with their start and end apart: 12, of which 10 were waited for; matrix products, arithmetic and copies ran while one was open for 12% of the time, Pallas kernels for 0%

commit v1 on v0

--- a/solution.py
+++ b/solution.py
@@ -106,7 +106,16 @@
     qkv_full = lax.all_gather(w_qkv, "fsdp", axis=0, tiled=True)
     out_full = lax.all_gather(w_out, "fsdp", axis=0, tiled=True)
     up_full = lax.all_gather(w_up, "fsdp", axis=0, tiled=True)
-    down_full = lax.all_gather(w_down, "fsdp", axis=0, tiled=True)
+    array = w_down
+    ways, here, step = (lax.axis_size("fsdp"), lax.axis_index("fsdp"), array.shape[0])
+    shape = [n * ways if d == 0 else n for d, n in enumerate(array.shape)]
+    full = lax.dynamic_update_slice_in_dim(
+        jnp.zeros(shape, array.dtype), array, here * step, axis=0
+    )
+    for far in range(1, ways):
+        array = lax.ppermute(array, "fsdp", [(d, (d + 1) % ways) for d in range(ways)])
+        full = lax.dynamic_update_slice_in_dim(full, array, (here - far) % ways * step, axis=0)
+    down_full = full
     normed_one, inverse_one = normalize(inputs)
     attn_in = (normed_one * (1.0 + scale_one) + shift_one).astype(bf16)
     qkv_bias = jnp.concatenate([query_bias, jnp.zeros_like(query_bias), value_bias]).astype(f32)

time: 444 us -> 444 us (level); the launches traced: 443 us -> 438 us
  waiting for transfers between devices: 268 us -> 250 us
  local copies, waits for them, and re-layouts: 38.8 us -> 53.4 us
    ppermute x0 -> x15, waiting for transfers between devices: none -> 122 us  [body(): lax.ppermute(array, 'fsdp', [(d, (d + 1) % ways) for d in range(ways)])]
    all_gather x1 -> x0, waiting for transfers between devices: 51.3 us -> none  [body(): down_full = lax.all_gather(w_down, 'fsdp', axis=0, tiled=True)]
    all_gather x1, waiting for transfers between devices: 48.2 us -> 0.02 us  [body(): up_full = lax.all_gather(w_up, 'fsdp', axis=0, tiled=True)]
    all_gather x1, waiting for transfers between devices: 17.1 us -> 0.01 us  [body(): out_full = lax.all_gather(w_out, 'fsdp', axis=0, tiled=True)]
    dynamic_update_slice x0 -> x16, local copies, waits for them, and re-layouts: none -> 15.7 us  [the longest x15 15 us: body(): lax.dynamic_update_slice_in_dim(full, array, (here - far) % ways * step,...]
    all_to_all x1, waiting for transfers between devices: 13.7 us -> 0.01 us  [body(): lax.all_to_all(mod_part.reshape(fsdp_count, own_latents * 6 * D), 'fsdp',...]
    all_to_all x1, waiting for transfers between devices: 6.41 us -> 0.01 us  [body(): lax.all_to_all(cotangent, 'sp', split_axis=0, concat_axis=1, tiled=True)]
    unnamed x55 -> x59, local copies, waits for them, and re-layouts: 12.7 us -> 11 us
  transfers between devices with their start and end apart: 12 -> 26, of which waited for: 10 -> 18; matrix products, arithmetic and copies ran while one was open for 12% -> 15% of each run, Pallas kernels for 0% -> 0%
where the time goes in v1:
time: 444 us; the launch traced here: 438 us
  waiting for transfers between devices  250 us (56%)
  matrix products  54.1 us (12%)
  local copies, waits for them, and re-layouts  53.4 us (12%)
  starting transfers between devices  27.8 us (6%)
  blocking collectives  22.8 us (5%)
  between operations  15.1 us (3%)
  other arithmetic  14.9 us (3%)
    ppermute x15, waiting for transfers between devices, body(): lax.ppermute(array, 'fsdp', [(d, (d + 1) % ways) for d in range(ways)])  122 us
    unnamed x5, waiting for transfers between devices  94.9 us
    all_gather x1, blocking collectives, body(): lax.all_gather(jnp.concatenate(small).reshape(1, padded // 128, 128), 'fs...  22.8 us
    all_to_all x1, waiting for transfers between devices, body(): lax.all_to_all(jnp.broadcast_to(grad_mod[None], (owners, own_latents, 6 *...  18.5 us
    dynamic_update_slice x15, local copies, waits for them, and re-layouts, body(): lax.dynamic_update_slice_in_dim(full, array, (here - far) % ways * step,...  15 us
    unnamed x59, local copies, waits for them, and re-layouts  11 us
  transfers between devices with their start and end apart: 26, of which 18 were waited for; matrix products, arithmetic and copies ran while one was open for 15% of the time, Pallas kernels for 0%

profile of v1, /device:TPU:0, one launch (start us, length us, event | category | flops | bytes accessed | tf_op | source)
XLA Modules:
  0.0 437.9 jit_solution(11525001162575732519)
XLA Ops:
  10.0 3.8 all-to-all-start
  14.4 4.1 concatenate.24
  18.5 22.8 %all_gather.12 = bf16[16,32,128]{2,1,0:T(8,128)(2,1)S(1)} all-gather(bf16[1,32,128]{2,1,0:T(8,128)(2,1)S(1)} %bitcast.188), channel_id=1, replica_groups=mesh['fsdp'=16,'sp'=2] {'fsdp'}, dimensions={0}, use_global_device_ids=true | all-gather | bytes 139264 | tf_op jit(solution)/shard_map/all_gather | solution.py:74
  42.0 14.3 %collective-permute-done.1 = bf16[192,768]{1,0:T(8,128)(2,1)S(1)} collective-permute-done((bf16[192,768]{1,0:T(8,128)(2,1)S(1)}, bf16[192,768]{1,0:T(8,128)(2,1)S(1)}, u32[]{:S(2)}, u32[]{:S(2)}) %collective-permute-start.1) | collective-permute-done | bytes 294944 | tf_op jit(solution)/shard_map/ppermute | solution.py:116
  56.7 10.0 %collective-permute-done.2 = bf16[192,768]{1,0:T(8,128)(2,1)S(1)} collective-permute-done((bf16[192,768]{1,0:T(8,128)(2,1)S(1)}, bf16[192,768]{1,0:T(8,128)(2,1)S(1)}, u32[]{:S(2)}, u32[]{:S(2)}) %collective-permute-start.2) | collective-permute-done | bytes 294944 | tf_op jit(solution)/shard_map/ppermute | solution.py:116
  66.7 8.7 %collective-permute-done.3 = bf16[192,768]{1,0:T(8,128)(2,1)S(1)} collective-permute-done((bf16[192,768]{1,0:T(8,128)(2,1)S(1)}, bf16[192,768]{1,0:T(8,128)(2,1)S(1)}, u32[]{:S(2)}, u32[]{:S(2)}) %collective-permute-start.3) | collective-permute-done | bytes 294944 | tf_op jit(solution)/shard_map/ppermute | solution.py:116
  75.7 9.9 %collective-permute-done.4 = bf16[192,768]{1,0:T(8,128)(2,1)S(1)} collective-permute-done((bf16[192,768]{1,0:T(8,128)(2,1)S(1)}, bf16[192,768]{1,0:T(8,128)(2,1)S(1)}, u32[]{:S(2)}, u32[]{:S(2)}) %collective-permute-start.4) | collective-permute-done | bytes 294944 | tf_op jit(solution)/shard_map/ppermute | solution.py:116
  85.9 1.0 copy.104
  87.3 2.5 broadcast_in_dim.12
  90.5 5.9 %all-to-all-start.1 = ((f32[16,1,4608]{2,1,0:T(1,128)}), f32[16,1,4608]{2,1,0:T(1,128)S(1)}, u32[]{:S(2)}, u32[]{:S(2)}) async-start(f32[16,1,4608]{2,1,0:T(1,128)} %copy.104), calls=%async_computation.1 | async-start | bytes 589824 | tf_op jit(solution)/shard_map/all_to_all | solution.py:95
  97.2 14.1 %collective-permute-done.6 = bf16[192,768]{1,0:T(8,128)(2,1)} collective-permute-done((bf16[192,768]{1,0:T(8,128)(2,1)}, bf16[192,768]{1,0:T(8,128)(2,1)}, u32[]{:S(2)}, u32[]{:S(2)}) %collective-permute-start.6) | collective-permute-done | bytes 294944 | tf_op jit(solution)/shard_map/ppermute | solution.py:116
  112.1 3.5 all-to-all-start.3
  115.9 4.7 %collective-permute-done.7 = bf16[192,768]{1,0:T(8,128)(2,1)} collective-permute-done((bf16[192,768]{1,0:T(8,128)(2,1)}, bf16[192,768]{1,0:T(8,128)(2,1)}, u32[]{:S(2)}, u32[]{:S(2)}) %collective-permute-start.7) | collective-permute-done | bytes 294944 | tf_op jit(solution)/shard_map/ppermute | solution.py:116
  120.9 14.5 %collective-permute-done.8 = bf16[192,768]{1,0:T(8,128)(2,1)S(1)} collective-permute-done((bf16[192,768]{1,0:T(8,128)(2,1)}, bf16[192,768]{1,0:T(8,128)(2,1)S(1)}, u32[]{:S(2)}, u32[]{:S(2)}) %collective-permute-start.8) | collective-permute-done | bytes 294944 | tf_op jit(solution)/shard_map/ppermute | solution.py:116
  135.6 1.0 fusion.43
  136.6 9.5 %collective-permute-done.9 = bf16[192,768]{1,0:T(8,128)(2,1)} collective-permute-done((bf16[192,768]{1,0:T(8,128)(2,1)S(1)}, bf16[192,768]{1,0:T(8,128)(2,1)}, u32[]{:S(2)}, u32[]{:S(2)}) %collective-permute-start.9) | collective-permute-done | bytes 294944 | tf_op jit(solution)/shard_map/ppermute | solution.py:116
  147.7 12.4 %collective-permute-done.10 = bf16[192,768]{1,0:T(8,128)(2,1)S(1)} collective-permute-done((bf16[192,768]{1,0:T(8,128)(2,1)}, bf16[192,768]{1,0:T(8,128)(2,1)S(1)}, u32[]{:S(2)}, u32[]{:S(2)}) %collective-permute-start.10) | collective-permute-done | bytes 294944 | tf_op jit(solution)/shard_map/ppermute | solution.py:116
  162.4 7.4 %collective-permute-done.11 = bf16[192,768]{1,0:T(8,128)(2,1)S(1)} collective-permute-done((bf16[192,768]{1,0:T(8,128)(2,1)S(1)}, bf16[192,768]{1,0:T(8,128)(2,1)S(1)}, u32[]{:S(2)}, u32[]{:S(2)}) %collective-permute-start.11) | collective-permute-done | bytes 294944 | tf_op jit(solution)/shard_map/ppermute | solution.py:116
  169.8 1.7 constant_dynamic-update-slice_fusion.17
  171.5 1.7 constant_dynamic-update-slice_fusion.16
  173.2 1.7 constant_dynamic-update-slice_fusion.15
  174.9 3.8 collective-permute-done.12
  179.4 1.7 constant_dynamic-update-slice_fusion.13
  181.8 5.7 %collective-permute-done.13 = bf16[192,768]{1,0:T(8,128)(2,1)S(1)} collective-permute-done((bf16[192,768]{1,0:T(8,128)(2,1)S(1)}, bf16[192,768]{1,0:T(8,128)(2,1)S(1)}, u32[]{:S(2)}, u32[]{:S(2)}) %collective-permute-start.13) | collective-permute-done | bytes 294944 | tf_op jit(solution)/shard_map/ppermute | solution.py:116
  189.7 6.7 %collective-permute-done.14 = bf16[192,768]{1,0:T(8,128)(2,1)S(1)} collective-permute-done((bf16[192,768]{1,0:T(8,128)(2,1)S(1)}, bf16[192,768]{1,0:T(8,128)(2,1)S(1)}, u32[]{:S(2)}, u32[]{:S(2)}) %collective-permute-start.14) | collective-permute-done | bytes 294944 | tf_op jit(solution)/shard_map/ppermute | solution.py:116
  197.1 4.1 fusion.3
  201.2 2.0 copy.105
  203.2 2.2 fusion.60
  205.5 4.8 %convolution_convert_fusion.4 = bf16[12,256,64]{1,2,0:T(8,128)(2,1)} fusion(f32[12,256,256]{1,2,0:T(8,128)} %fusion.60, bf16[3,1,12,256,64]{3,4,2,1,0:T(8,128)(2,1)S(1)} %bitcast.160), kind=kOutput, calls=%fused_computation.34 | convolution fusion | flops 104008960 | bytes 7077888 | tf_op jit(solution)/shard_map/bhqk,bhkd->bhqd/dot_general | solution.py:133
  210.2 2.8 fusion.83
  213.3 4.0 convolution_add_fusion.1
  217.3 6.4 %fusion.80 = (bf16[3072]{0:T(1024)(128)(2,1)S(1)}, bf16[256,3072]{1,0:T(8,128)(2,1)S(1)}) fusion(f32[256,3072]{1,0:T(8,128)S(1)} %convolution_add_fusion.1, bf16[256,768]{1,0:T(8,128)(2,1)S(1)} %copy-done.12, bf16[3072,768]{1,0:T(8,128)(2,1)} %constant_dynamic-update-slice_fusion.8), kind=kOutput, calls=%fused_computation.169 | convolution fusion | flops 1224471552 | bytes 9836544 | tf_op jit(solution)/shard_map/btd,fd->btf/dot_general | solution.py:156
  223.7 1.4 fusion.86
  225.2 5.2 %fusion.25 = (f32[768]{0:T(1024)S(1)}, bf16[1,256,768]{2,1,0:T(8,128)(2,1)}, f32[768]{0:T(1024)S(1)}, f32[256]{0:T(256)S(1)}, f32[256]{0:T(256)S(1)}, /*index=5*/f32[768]{0:T(1024)S(1)}) fusion(bf16[2,128,768]{2,1,0:T(8,128)(2,1)S(1)} %all-to-all-done.3, f32[256,768]{1,0:T(8,128)S(1)} %get-tuple-element.36, f32[768]{0:T(1024)S(1)} %get-tuple-element.24, ...), kind=kOutput, calls=%fused_computation.51 | convolution fusion | flops 1218180352 | bytes 10246144 | tf_op jit(solution)/shard_map/btf,fd->btd/dot_general | solution.py:147
  230.4 1.3 fusion.82
  233.0 0.9 copy.109
  233.9 4.8 %fusion.20 = bf16[1,1,12,256,64]{3,4,2,1,0:T(8,128)(2,1)} fusion(bf16[12,256,64]{1,2,0:T(8,128)(2,1)} %bitcast.174, f32[12,256,256]{1,2,0:T(8,128)} %fusion.60), kind=kOutput, calls=%fused_computation.39 | convolution fusion | flops 104008960 | bytes 3932160 | tf_op jit(solution)/shard_map/bhqk,bhqd->bhkd/dot_general | solution.py:183
  239.5 1.1 copy-done.1
  240.6 2.6 multiply_reduce_fusion
  244.9 1.0 copy-done.20
  245.9 2.3 convolution_convert_fusion.2
  248.2 2.3 copy.117
  250.5 1.0 copy.132
  251.6 2.5 constant_dynamic-update-slice_fusion.7
  254.1 3.8 fusion.2
  258.0 3.0 fusion.1
  261.0 1.5 fusion.17
  264.3 1.0 copy-done.14
  266.4 3.2 reduce.65
  270.5 3.5 all-to-all-start.2
  274.0 3.9 fusion.39
  278.4 1.7 copy.113
  281.0 3.6 all-to-all-start.4
  284.7 7.9 %all-to-all-done.4 = f32[1,256,768]{2,0,1:T(1,128)S(1)} async-done(((f32[1,256,768]{2,0,1:T(1,128)}), f32[1,256,768]{2,0,1:T(1,128)S(1)}, u32[]{:S(2)}, u32[]{:S(2)}) %all-to-all-start.4) | async-done | bytes 786464 | tf_op jit(solution)/shard_map/all_to_all | solution.py:199
  292.5 1.1 broadcast_in_dim.14
  293.7 2.6 all-to-all-start.5
  297.9 0.9 copy.127
  298.9 18.5 %all-to-all-done.5 = f32[32,1,4608]{2,1,0:T(1,128)S(1)} async-done(((f32[32,1,4608]{2,1,0:T(1,128)}), f32[32,1,4608]{2,1,0:T(1,128)S(1)}, u32[]{:S(2)}, u32[]{:S(2)}) %all-to-all-start.5) | async-done | bytes 589856 | tf_op jit(solution)/shard_map/all_to_all | solution.py:211
  318.2 3.5 all-to-all-start.6
  322.2 1.3 fusion.46
  324.1 5.9 %all-to-all-done.6 = f32[16,1,96]{2,1,0:T(1,128)S(1)} async-done(((f32[16,1,96]{2,1,0:T(1,128)}), f32[16,1,96]{2,1,0:T(1,128)S(1)}, u32[]{:S(2)}, u32[]{:S(2)}) %all-to-all-start.6) | async-done | bytes 6176 | tf_op jit(solution)/shard_map/all_to_all | solution.py:265
  332.0 92.8 %reduce-scatter.4.cloned.1.call-done = bf16[24,9344]{1,0:T(8,128)(2,1)} async-done(((bf16[768,9344]{1,0:T(8,128)(2,1)}), bf16[24,9344]{1,0:T(8,128)(2,1)}) %reduce-scatter.4.cloned.1.call-update) | async-done | bytes 448528
  424.8 1.1 convert_element_type.313
  427.1 1.7 fusion.84
  (177 shorter events, 34.5 us)
Async XLA Ops:
  7.2 68.3 %copy-start = (bf16[48,4608]{1,0:T(8,128)(2,1)S(1)}, bf16[48,4608]{1,0:T(8,128)(2,1)}, u32[]{:S(2)}) copy-start(bf16[48,4608]{1,0:T(8,128)(2,1)} %param.17) | copy-start | bytes 1327108
  7.2 189.9 %all-gather.4.cloned.1.call-start = ((), (), s32[]{:S(2)}) async-start(), calls=%async_computation.8 | async-start | bytes 3760128 | tf_op jit(solution)/shard_map/all_gather | solution.py:106
  7.9 202.3 %all-gather.6.cloned.1.call-start = ((), (), s32[]{:S(2)}) async-start(), calls=%async_computation.9 | async-start | bytes 1253376 | tf_op jit(solution)/shard_map/all_gather | solution.py:107
  8.7 204.6 %all-gather.8.cloned.1.call-start = ((), (), s32[]{:S(2)}) async-start(), calls=%async_computation.10 | async-start | bytes 5013504 | tf_op jit(solution)/shard_map/all_gather | solution.py:108
  9.4 32.0 %collective-permute-start = (bf16[192,768]{1,0:T(8,128)(2,1)}, bf16[192,768]{1,0:T(8,128)(2,1)S(1)}, u32[]{:S(2)}, u32[]{:S(2)}) collective-permute-start(bf16[192,768]{1,0:T(8,128)(2,1)} %param.26), channel_id=1, source_target_pairs={{0,2},{2,4},{4,6},{6,8},{8,10},{10,12},{12,14},{14,16},{16,18},{18... | collective-permute-start | bytes 884744 | tf_op jit(solution)/shard_map/ppermute | solution.py:116
  10.0 80.5 %all-to-all-start = ((bf16[2,128,768]{2,1,0:T(8,128)(2,1)}), bf16[2,128,768]{2,1,0:T(8,128)(2,1)S(1)}, u32[]{:S(2)}, u32[]{:S(2)}) async-start(bf16[2,128,768]{2,1,0:T(8,128)(2,1)} %param.14), calls=%async_computation | async-start | bytes 786432 | tf_op jit(solution)/shard_map/all_to_all | solution.py:85
  41.4 14.8 %collective-permute-start.1 = (bf16[192,768]{1,0:T(8,128)(2,1)S(1)}, bf16[192,768]{1,0:T(8,128)(2,1)S(1)}, u32[]{:S(2)}, u32[]{:S(2)}) collective-permute-start(bf16[192,768]{1,0:T(8,128)(2,1)S(1)} %collective-permute-done), channel_id=1, source_target_pairs={{0,2},{2,4},{4,6},{6,8},{8,10},{10,12},{12,14},{14,16},{16,18},{18... | collective-permute-start | bytes 884744 | tf_op jit(solution)/shard_map/ppermute | solution.py:116
  56.3 10.4 %collective-permute-start.2 = (bf16[192,768]{1,0:T(8,128)(2,1)S(1)}, bf16[192,768]{1,0:T(8,128)(2,1)S(1)}, u32[]{:S(2)}, u32[]{:S(2)}) collective-permute-start(bf16[192,768]{1,0:T(8,128)(2,1)S(1)} %collective-permute-done.1), channel_id=1, source_target_pairs={{0,2},{2,4},{4,6},{6,8},{8,10},{10,12},{12,14},{14,16},{16,18},{18... | collective-permute-start | bytes 884744 | tf_op jit(solution)/shard_map/ppermute | solution.py:116
  66.6 8.8 %collective-permute-start.3 = (bf16[192,768]{1,0:T(8,128)(2,1)S(1)}, bf16[192,768]{1,0:T(8,128)(2,1)S(1)}, u32[]{:S(2)}, u32[]{:S(2)}) collective-permute-start(bf16[192,768]{1,0:T(8,128)(2,1)S(1)} %collective-permute-done.2), channel_id=1, source_target_pairs={{0,2},{2,4},{4,6},{6,8},{8,10},{10,12},{12,14},{14,16},{16,18},{18... | collective-permute-start | bytes 884744 | tf_op jit(solution)/shard_map/ppermute | solution.py:116
  75.5 10.1 %collective-permute-start.4 = (bf16[192,768]{1,0:T(8,128)(2,1)S(1)}, bf16[192,768]{1,0:T(8,128)(2,1)S(1)}, u32[]{:S(2)}, u32[]{:S(2)}) collective-permute-start(bf16[192,768]{1,0:T(8,128)(2,1)S(1)} %collective-permute-done.3), channel_id=1, source_target_pairs={{0,2},{2,4},{4,6},{6,8},{8,10},{10,12},{12,14},{14,16},{16,18},{18... | collective-permute-start | bytes 884744 | tf_op jit(solution)/shard_map/ppermute | solution.py:116
  75.7 14.1 %copy-start.15 = (bf16[192,768]{1,0:T(8,128)(2,1)S(1)}, bf16[192,768]{1,0:T(8,128)(2,1)}, u32[]{:S(2)}) copy-start(bf16[192,768]{1,0:T(8,128)(2,1)} %param.26) | copy-start | bytes 884740
  85.6 10.9 %collective-permute-start.5 = (bf16[192,768]{1,0:T(8,128)(2,1)S(1)}, bf16[192,768]{1,0:T(8,128)(2,1)}, u32[]{:S(2)}, u32[]{:S(2)}) collective-permute-start(bf16[192,768]{1,0:T(8,128)(2,1)S(1)} %collective-permute-done.4), channel_id=1, source_target_pairs={{0,2},{2,4},{4,6},{6,8},{8,10},{10,12},{12,14},{14,16},{16,18},{18... | collective-permute-start | bytes 884744 | tf_op jit(solution)/shard_map/ppermute | solution.py:116
  90.5 21.7 %all-to-all-start.1 = ((f32[16,1,4608]{2,1,0:T(1,128)}), f32[16,1,4608]{2,1,0:T(1,128)S(1)}, u32[]{:S(2)}, u32[]{:S(2)}) async-start(f32[16,1,4608]{2,1,0:T(1,128)} %copy.104), calls=%async_computation.1 | async-start | bytes 589824 | tf_op jit(solution)/shard_map/all_to_all | solution.py:95
  96.5 14.9 %collective-permute-start.6 = (bf16[192,768]{1,0:T(8,128)(2,1)}, bf16[192,768]{1,0:T(8,128)(2,1)}, u32[]{:S(2)}, u32[]{:S(2)}) collective-permute-start(bf16[192,768]{1,0:T(8,128)(2,1)} %collective-permute-done.5), channel_id=1, source_target_pairs={{0,2},{2,4},{4,6},{6,8},{8,10},{10,12},{12,14},{14,16},{16,18},{18... | collective-permute-start | bytes 884744 | tf_op jit(solution)/shard_map/ppermute | solution.py:116
  111.3 9.2 %collective-permute-start.7 = (bf16[192,768]{1,0:T(8,128)(2,1)}, bf16[192,768]{1,0:T(8,128)(2,1)}, u32[]{:S(2)}, u32[]{:S(2)}) collective-permute-start(bf16[192,768]{1,0:T(8,128)(2,1)} %collective-permute-done.6), channel_id=1, source_target_pairs={{0,2},{2,4},{4,6},{6,8},{8,10},{10,12},{12,14},{14,16},{16,18},{18... | collective-permute-start | bytes 884744 | tf_op jit(solution)/shard_map/ppermute | solution.py:116
  112.1 23.3 %all-to-all-start.3 = ((bf16[2,128,768]{2,1,0:T(8,128)(2,1)}), bf16[2,128,768]{2,1,0:T(8,128)(2,1)S(1)}, u32[]{:S(2)}, u32[]{:S(2)}) async-start(bf16[2,128,768]{2,1,0:T(8,128)(2,1)} %param.16), calls=%async_computation.3 | async-start | bytes 786432 | tf_op jit(solution)/shard_map/all_to_all | solution.py:86
  115.6 309.2 %reduce-scatter.4.cloned.1.call-start = ((), (), s32[]{:S(2)}) async-start(), calls=%async_computation.11 | async-start | bytes 14800896
  120.6 14.8 %collective-permute-start.8 = (bf16[192,768]{1,0:T(8,128)(2,1)}, bf16[192,768]{1,0:T(8,128)(2,1)S(1)}, u32[]{:S(2)}, u32[]{:S(2)}) collective-permute-start(bf16[192,768]{1,0:T(8,128)(2,1)} %collective-permute-done.7), channel_id=1, source_target_pairs={{0,2},{2,4},{4,6},{6,8},{8,10},{10,12},{12,14},{14,16},{16,18},{18... | collective-permute-start | bytes 884744 | tf_op jit(solution)/shard_map/ppermute | solution.py:116
  135.4 10.8 %collective-permute-start.9 = (bf16[192,768]{1,0:T(8,128)(2,1)S(1)}, bf16[192,768]{1,0:T(8,128)(2,1)}, u32[]{:S(2)}, u32[]{:S(2)}) collective-permute-start(bf16[192,768]{1,0:T(8,128)(2,1)S(1)} %collective-permute-done.8), channel_id=1, source_target_pairs={{0,2},{2,4},{4,6},{6,8},{8,10},{10,12},{12,14},{14,16},{16,18},{18... | collective-permute-start | bytes 884744 | tf_op jit(solution)/shard_map/ppermute | solution.py:116
  146.2 13.9 %collective-permute-start.10 = (bf16[192,768]{1,0:T(8,128)(2,1)}, bf16[192,768]{1,0:T(8,128)(2,1)S(1)}, u32[]{:S(2)}, u32[]{:S(2)}) collective-permute-start(bf16[192,768]{1,0:T(8,128)(2,1)} %collective-permute-done.9), channel_id=1, source_target_pairs={{0,2},{2,4},{4,6},{6,8},{8,10},{10,12},{12,14},{14,16},{16,18},{18... | collective-permute-start | bytes 884744 | tf_op jit(solution)/shard_map/ppermute | solution.py:116
  160.1 9.7 %collective-permute-start.11 = (bf16[192,768]{1,0:T(8,128)(2,1)S(1)}, bf16[192,768]{1,0:T(8,128)(2,1)S(1)}, u32[]{:S(2)}, u32[]{:S(2)}) collective-permute-start(bf16[192,768]{1,0:T(8,128)(2,1)S(1)} %collective-permute-done.10), channel_id=1, source_target_pairs={{0,2},{2,4},{4,6},{6,8},{8,10},{10,12},{12,14},{14,16},{16,18},{18... | collective-permute-start | bytes 884744 | tf_op jit(solution)/shard_map/ppermute | solution.py:116
  169.8 8.8 %collective-permute-start.12 = (bf16[192,768]{1,0:T(8,128)(2,1)S(1)}, bf16[192,768]{1,0:T(8,128)(2,1)S(1)}, u32[]{:S(2)}, u32[]{:S(2)}) collective-permute-start(bf16[192,768]{1,0:T(8,128)(2,1)S(1)} %collective-permute-done.11), channel_id=1, source_target_pairs={{0,2},{2,4},{4,6},{6,8},{8,10},{10,12},{12,14},{14,16},{16,18},{18... | collective-permute-start | bytes 884744 | tf_op jit(solution)/shard_map/ppermute | solution.py:116
  178.6 8.8 %collective-permute-start.13 = (bf16[192,768]{1,0:T(8,128)(2,1)S(1)}, bf16[192,768]{1,0:T(8,128)(2,1)S(1)}, u32[]{:S(2)}, u32[]{:S(2)}) collective-permute-start(bf16[192,768]{1,0:T(8,128)(2,1)S(1)} %collective-permute-done.12), channel_id=1, source_target_pairs={{0,2},{2,4},{4,6},{6,8},{8,10},{10,12},{12,14},{14,16},{16,18},{18... | collective-permute-start | bytes 884744 | tf_op jit(solution)/shard_map/ppermute | solution.py:116
  187.5 8.8 %collective-permute-start.14 = (bf16[192,768]{1,0:T(8,128)(2,1)S(1)}, bf16[192,768]{1,0:T(8,128)(2,1)S(1)}, u32[]{:S(2)}, u32[]{:S(2)}) collective-permute-start(bf16[192,768]{1,0:T(8,128)(2,1)S(1)} %collective-permute-done.13), channel_id=1, source_target_pairs={{0,2},{2,4},{4,6},{6,8},{8,10},{10,12},{12,14},{14,16},{16,18},{18... | collective-permute-start | bytes 884744 | tf_op jit(solution)/shard_map/ppermute | solution.py:116
  213.3 4.0 copy-start.12
  213.3 10.4 %slice-start = ((s8[4718592]{0:T(1024)(128)(4,1)}), s8[4194304]{0:T(1024)(128)(4,1)S(1)}, s32[]{:S(2)}) async-start(s8[4718592]{0:T(1024)(128)(4,1)} %bitcast.190), calls=%async_computation.12 | async-start | bytes 8388608
  217.3 7.9 %copy-start.19 = (f32[256,3072]{1,0:T(8,128)}, f32[256,3072]{1,0:T(8,128)S(1)}, u32[]{:S(2)}) copy-start(f32[256,3072]{1,0:T(8,128)S(1)} %convolution_add_fusion.1) | copy-start | bytes 9437188
  217.3 6.4 %slice-start.1 = ((s8[4718592]{0:T(1024)(128)(4,1)}), s8[524288]{0:T(1024)(128)(4,1)S(1)}, s32[]{:S(2)}) async-start(s8[4718592]{0:T(1024)(128)(4,1)} %bitcast.190), calls=%async_computation.13 | async-start | bytes 1048576
  223.7 1.5 copy-start.17
  230.4 2.0 copy-start.2
  231.7 0.7 copy-start.4
  233.9 4.8 %copy-start.9 = (bf16[256,768]{0,1:T(8,128)(2,1)S(1)}, bf16[256,768]{0,1:T(8,128)(2,1)}, u32[]{:S(2)}) copy-start(bf16[256,768]{0,1:T(8,128)(2,1)} %copy.109) | copy-start | bytes 1179652
  238.7 1.9 copy-start.1
  243.9 1.0 copy-start.13
  243.9 2.0 copy-start.20
  251.6 2.5 copy-start.18
  254.1 3.8 copy-start.10
  254.1 3.9 copy-start.11
  258.0 3.0 copy-start.5
  258.0 3.0 copy-start.8
  264.3 1.0 copy-start.14
  270.5 10.5 %all-to-all-start.2 = ((bf16[2,2,49152]{2,1,0:T(2,128)(2,1)}), bf16[2,2,49152]{2,1,0:T(2,128)(2,1)S(1)}, u32[]{:S(2)}, u32[]{:S(2)}) async-start(bf16[2,2,49152]{2,1,0:T(2,128)(2,1)} %reshape.781), calls=%async_computation.2 | async-start | bytes 786432 | tf_op jit(solution)/shard_map/all_to_all | solution.py:151
  274.0 3.9 copy-start.6
  274.0 3.9 copy-start.7
  281.0 11.6 %all-to-all-start.4 = ((f32[1,256,768]{2,0,1:T(1,128)}), f32[1,256,768]{2,0,1:T(1,128)S(1)}, u32[]{:S(2)}, u32[]{:S(2)}) async-start(f32[1,256,768]{2,0,1:T(1,128)} %copy.113), calls=%async_computation.4 | async-start | bytes 1572864 | tf_op jit(solution)/shard_map/all_to_all | solution.py:199
  293.7 23.7 %all-to-all-start.5 = ((f32[32,1,4608]{2,1,0:T(1,128)}), f32[32,1,4608]{2,1,0:T(1,128)S(1)}, u32[]{:S(2)}, u32[]{:S(2)}) async-start(f32[32,1,4608]{2,1,0:T(1,128)} %broadcast_in_dim.14), calls=%async_computation.5 | async-start | bytes 1179648 | tf_op jit(solution)/shard_map/all_to_all | solution.py:211
  296.7 34.7 %copy-start.16 = (bf16[2,768]{1,0:T(2,128)(2,1)S(1)}, bf16[2,768]{1,0:T(2,128)(2,1)}, u32[]{:S(2)}) copy-start(bf16[2,768]{1,0:T(2,128)(2,1)} %param.15) | copy-start | bytes 9220
  318.2 11.8 %all-to-all-start.6 = ((f32[16,1,96]{2,1,0:T(1,128)}), f32[16,1,96]{2,1,0:T(1,128)S(1)}, u32[]{:S(2)}, u32[]{:S(2)}) async-start(f32[16,1,96]{2,1,0:T(1,128)} %bitcast.29), calls=%async_computation.6 | async-start | bytes 16384 | tf_op jit(solution)/shard_map/all_to_all | solution.py:265
  424.8 5.0 %copy-start.3 = (bf16[24,9344]{1,0:T(8,128)(2,1)S(1)}, bf16[24,9344]{1,0:T(8,128)(2,1)}, u32[]{:S(2)}) copy-start(bf16[24,9344]{1,0:T(8,128)(2,1)} %reduce-scatter.4.cloned.1.call-done) | copy-start | bytes 1345540
Sparse Core Ops, SparseCore 0:
  10.3 52.2 all-gather.3
  64.9 41.7 all-gather.5
  109.0 58.7 all-gather.7
  264.5 160.2 reduce-scatter.3
